TPU v7x, 512 devices: a whole 4x4x16 slice. The times are simulated.
512 devices in a mesh: bulk: 32 (over z, core), blk: 16 (over y, x).
Axes of the slice: x: 4, y: 4, z: 16, core: 2. Of those that a mesh axis runs over, the one named last changes fastest.
Arguments:
- factor: float32 [131072, 4096], P(('bulk', 'blk')), parts along dimension 0, as said below
- initial: float32 [131072, 128], P(('bulk', 'blk')), parts along dimension 0, may hold values from -6 to 6
- bounds: float32 [64], P('bulk'), parts along dimension 0, may hold values from 0 to 15.5, as said below
Outputs:
- basis_rows: float32 [131072, 128], P(('bulk', 'blk')), parts along dimension 0
- projected: float32 [4096, 128], P('bulk'), parts along dimension 0
- residual: float32 [131072, 128], P(('bulk', 'blk')), parts along dimension 0
There are 32 independent parts, one for each index of `bulk`. A program takes and returns all parts, laid end to end along the dimension named above; each array names one. Nothing has to cross between parts.
Inputs may be any that keep to these rules, and one draw needn't show every extreme that they name: factor is symmetric. `bounds`: the upper end exceeds the lower end by 14 or more.
All inputs are finite; a program needn't handle non-finite values.
Results may differ from a plain program's by a relative error of at most 0.0003.
Values sent between devices are 32-bit elements; how exact they have to be, the bound alone decides.
A program may use at most 64 MiB of HBM per device.

v0:
```python
import jax
import jax.numpy as jnp
from jax import lax
from jax.sharding import PartitionSpec as P

DEGREE = 8


def local_dot(left_side, right_side):
    return jnp.dot(
        left_side, right_side, precision=lax.Precision.HIGHEST, preferred_element_type=jnp.float32
    )


def lower_solve(cholesky_low, right_side):
    return lax.linalg.triangular_solve(cholesky_low, right_side, left_side=True, lower=True)


def apply_factor(factor_rows, vectors):
    return local_dot(factor_rows, lax.all_gather(vectors, "blk", axis=0, tiled=True))


def local(factor, initial, bounds):
    centre = (bounds[0] + bounds[1]) / 2.0
    radius = (bounds[1] - bounds[0]) / 2.0
    previous = initial
    current = (apply_factor(factor, initial) - centre * initial) / radius
    for order_step in range(DEGREE - 1):
        scaled = (apply_factor(factor, current) - centre * current) / radius
        following = 2.0 * scaled - previous
        previous = current
        current = following
    gram_matrix = lax.psum(
        lax.dot_general(
            current,
            current,
            (((0,), (0,)), ((), ())),
            precision=lax.Precision.HIGHEST,
            preferred_element_type=jnp.float32,
        ),
        "blk",
    )
    cholesky_low = jnp.linalg.cholesky(gram_matrix)
    basis_rows = lower_solve(cholesky_low, current.T).T
    mapped = apply_factor(factor, basis_rows)
    projected = lax.psum(
        lax.dot_general(
            basis_rows,
            mapped,
            (((0,), (0,)), ((), ())),
            precision=lax.Precision.HIGHEST,
            preferred_element_type=jnp.float32,
        ),
        "blk",
    )
    residual = mapped - local_dot(basis_rows, projected)
    return (basis_rows, projected, residual)


def solution(mesh):
    in_specs = (P(("bulk", "blk"), None), P(("bulk", "blk"), None), P("bulk"))
    out_specs = (P(("bulk", "blk"), None), P("bulk", None), P(("bulk", "blk"), None))
    return jax.shard_map(local, mesh=mesh, in_specs=in_specs, out_specs=out_specs, check_vma=False)
```

profile of v0, /device:TPU:2, one launch (start us, length us, event | category | flops | bytes accessed | tf_op | source)
XLA Modules:
  0.0 879.8 jit_solution(10453286735526572936)
XLA Ops:
  7.9 1.3 fusion.33
  11.9 63.6 %all-gather.10.cloned.1.call-done = f32[4096,128]{1,0:T(8,128)} async-done(((f32[256,128]{1,0:T(8,128)}), f32[4096,128]{1,0:T(8,128)}) %all-gather.10.cloned.1.call-update) | async-done | bytes 2097168 | tf_op jit(solution)/shard_map/all_gather | solution.py:20
  75.4 7.0 fusion.28
  82.5 59.8 %all-gather.12.cloned.1.call-done = f32[4096,128]{1,0:T(8,128)} async-done(((f32[256,128]{1,0:T(8,128)}), f32[4096,128]{1,0:T(8,128)}) %all-gather.12.cloned.1.call-update) | async-done | bytes 2097168 | tf_op jit(solution)/shard_map/all_gather | solution.py:20
  142.3 7.0 fusion.27
  149.3 59.8 %all-gather.14.cloned.1.call-done = f32[4096,128]{1,0:T(8,128)} async-done(((f32[256,128]{1,0:T(8,128)}), f32[4096,128]{1,0:T(8,128)}) %all-gather.14.cloned.1.call-update) | async-done | bytes 2097168 | tf_op jit(solution)/shard_map/all_gather | solution.py:20
  209.1 7.0 fusion.23
  216.6 59.3 %all-gather.16.cloned.1.call-done = f32[4096,128]{1,0:T(8,128)} async-done(((f32[256,128]{1,0:T(8,128)}), f32[4096,128]{1,0:T(8,128)}) %all-gather.16.cloned.1.call-update) | async-done | bytes 2097168 | tf_op jit(solution)/shard_map/all_gather | solution.py:20
  276.0 7.0 fusion.19
  283.0 59.8 %all-gather.18.cloned.1.call-done = f32[4096,128]{1,0:T(8,128)} async-done(((f32[256,128]{1,0:T(8,128)}), f32[4096,128]{1,0:T(8,128)}) %all-gather.18.cloned.1.call-update) | async-done | bytes 2097168 | tf_op jit(solution)/shard_map/all_gather | solution.py:20
  342.8 7.0 fusion.15
  349.9 59.8 %all-gather.20.cloned.1.call-done = f32[4096,128]{1,0:T(8,128)} async-done(((f32[256,128]{1,0:T(8,128)}), f32[4096,128]{1,0:T(8,128)}) %all-gather.20.cloned.1.call-update) | async-done | bytes 2097168 | tf_op jit(solution)/shard_map/all_gather | solution.py:20
  409.7 7.0 fusion.11
  416.9 59.6 %all-gather.22.cloned.1.call-done = f32[4096,128]{1,0:T(8,128)} async-done(((f32[256,128]{1,0:T(8,128)}), f32[4096,128]{1,0:T(8,128)}) %all-gather.22.cloned.1.call-update) | async-done | bytes 2097168 | tf_op jit(solution)/shard_map/all_gather | solution.py:20
  476.5 7.0 fusion.7
  483.6 59.8 %all-gather.24.cloned.1.call-done = f32[4096,128]{1,0:T(8,128)} async-done(((f32[256,128]{1,0:T(8,128)}), f32[4096,128]{1,0:T(8,128)}) %all-gather.24.cloned.1.call-update) | async-done | bytes 2097168 | tf_op jit(solution)/shard_map/all_gather | solution.py:20
  543.4 6.3 fusion.3
  551.0 111.0 %all-reduce.3.cloned.1.call-done = f32[128,128]{0,1:T(8,128)} async-done(((f32[128,128]{0,1:T(8,128)}), f32[128,128]{0,1:T(8,128)}) %all-reduce.3.cloned.1.call-update) | async-done | bytes 65552 | tf_op jit(solution)/shard_map/psum | solution.py:33
  663.8 11.7 %cholesky.16 = f32[128,128]{1,0:T(8,128)S(1)} custom-call(f32[128,128]{1,0:T(8,128)S(1)} %fusion.32), custom_call_target="Cholesky" | custom-call | tf_op jit(solution)/shard_map/jit(cholesky)/cholesky | solution.py:43
  676.8 9.8 %custom-call.6 = f32[1,128,128]{1,2,0:T(8,128)S(1)} custom-call(f32[1,128,128]{2,1,0:T(8,128)S(1)} %fusion.29), custom_call_target="InvertDiagBlocksLowerTriangular" | custom-call | tf_op jit(solution)/shard_map/triangular_solve | solution.py:16
  687.7 62.6 %all-gather.26.cloned.1.call-done = f32[4096,128]{0,1:T(8,128)} async-done(((f32[256,128]{0,1:T(8,128)}), f32[4096,128]{0,1:T(8,128)}) %all-gather.26.cloned.1.call-update) | async-done | bytes 2097168 | tf_op jit(solution)/shard_map/all_gather | solution.py:20
  750.3 7.1 fusion.35
  759.1 110.6 %all-reduce.5.cloned.1.call-done = f32[128,128]{1,0:T(8,128)} async-done(((f32[128,128]{1,0:T(8,128)}), f32[128,128]{1,0:T(8,128)}) %all-reduce.5.cloned.1.call-update) | async-done | bytes 65552 | tf_op jit(solution)/shard_map/psum | solution.py:46
  871.6 1.5 copy.29
  (49 shorter events, 10.9 us)
Async XLA Ops:
  7.2 68.3 %all-gather.10.cloned.1.call-start = ((), (), s32[]{:S(2)}) async-start(), calls=%async_computation | async-start | bytes 2228224 | tf_op jit(solution)/shard_map/all_gather | solution.py:20
  7.9 134.4 %all-gather.12.cloned.1.call-start = ((), (), s32[]{:S(2)}) async-start(), calls=%async_computation.1 | async-start | bytes 2228224 | tf_op jit(solution)/shard_map/all_gather | solution.py:20
  75.4 66.9 %copy-start.7 = (f32[256,128]{1,0:T(8,128)S(1)}, f32[256,128]{1,0:T(8,128)}, u32[]{:S(2)}) copy-start(f32[256,128]{1,0:T(8,128)} %param.4) | copy-start | bytes 393220
  82.4 126.7 %copy-start.6 = (f32[256,128]{1,0:T(8,128)S(1)}, f32[256,128]{1,0:T(8,128)}, u32[]{:S(2)}) copy-start(f32[256,128]{1,0:T(8,128)} %fusion.28) | copy-start | bytes 393220
  82.4 126.7 %all-gather.14.cloned.1.call-start = ((), (), s32[]{:S(2)}) async-start(), calls=%async_computation.2 | async-start | bytes 2228224 | tf_op jit(solution)/shard_map/all_gather | solution.py:20
  149.3 126.7 %copy-start.5 = (f32[256,128]{1,0:T(8,128)S(1)}, f32[256,128]{1,0:T(8,128)}, u32[]{:S(2)}) copy-start(f32[256,128]{1,0:T(8,128)} %fusion.27) | copy-start | bytes 393220
  149.3 126.7 %all-gather.16.cloned.1.call-start = ((), (), s32[]{:S(2)}) async-start(), calls=%async_computation.3 | async-start | bytes 2228224 | tf_op jit(solution)/shard_map/all_gather | solution.py:20
  216.1 126.7 %copy-start.2 = (f32[256,128]{1,0:T(8,128)S(1)}, f32[256,128]{1,0:T(8,128)}, u32[]{:S(2)}) copy-start(f32[256,128]{1,0:T(8,128)} %fusion.23) | copy-start | bytes 393220
  216.1 126.7 %all-gather.18.cloned.1.call-start = ((), (), s32[]{:S(2)}) async-start(), calls=%async_computation.4 | async-start | bytes 2228224 | tf_op jit(solution)/shard_map/all_gather | solution.py:20
  283.0 126.7 %copy-start.3 = (f32[256,128]{1,0:T(8,128)S(1)}, f32[256,128]{1,0:T(8,128)}, u32[]{:S(2)}) copy-start(f32[256,128]{1,0:T(8,128)} %fusion.19) | copy-start | bytes 393220
  283.0 126.7 %all-gather.20.cloned.1.call-start = ((), (), s32[]{:S(2)}) async-start(), calls=%async_computation.5 | async-start | bytes 2228224 | tf_op jit(solution)/shard_map/all_gather | solution.py:20
  349.8 126.7 %copy-start.4 = (f32[256,128]{1,0:T(8,128)S(1)}, f32[256,128]{1,0:T(8,128)}, u32[]{:S(2)}) copy-start(f32[256,128]{1,0:T(8,128)} %fusion.15) | copy-start | bytes 393220
  349.8 126.7 %all-gather.22.cloned.1.call-start = ((), (), s32[]{:S(2)}) async-start(), calls=%async_computation.6 | async-start | bytes 2228224 | tf_op jit(solution)/shard_map/all_gather | solution.py:20
  416.7 126.7 %copy-start.1 = (f32[256,128]{1,0:T(8,128)S(1)}, f32[256,128]{1,0:T(8,128)}, u32[]{:S(2)}) copy-start(f32[256,128]{1,0:T(8,128)} %fusion.11) | copy-start | bytes 393220
  416.7 126.7 %all-gather.24.cloned.1.call-start = ((), (), s32[]{:S(2)}) async-start(), calls=%async_computation.7 | async-start | bytes 2228224 | tf_op jit(solution)/shard_map/all_gather | solution.py:20
  483.5 178.5 %all-reduce.3.cloned.1.call-start = ((), (), s32[]{:S(2)}) async-start(), calls=%async_computation.8 | async-start | bytes 131072 | tf_op jit(solution)/shard_map/psum | solution.py:33
  550.7 199.6 %all-gather.26.cloned.1.call-start = ((), (), s32[]{:S(2)}) async-start(), calls=%async_computation.9 | async-start | bytes 2228224 | tf_op jit(solution)/shard_map/all_gather | solution.py:20
  687.7 69.7 %copy-start = (f32[128,256]{1,0:T(8,128)S(1)}, f32[128,256]{1,0:T(8,128)}, u32[]{:S(2)}) copy-start(f32[128,256]{1,0:T(8,128)} %fusion.30) | copy-start | bytes 393220
  687.7 182.0 %all-reduce.5.cloned.1.call-start = ((), (), s32[]{:S(2)}) async-start(), calls=%async_computation.10 | async-start | bytes 131072 | tf_op jit(solution)/shard_map/psum | solution.py:46
Sparse Core Ops, SparseCore 0:
  11.0 64.3 all-gather.9
  82.5 59.6 all-gather.11
  149.4 59.6 all-gather.13
  216.2 59.6 all-gather.15
  283.1 59.6 all-gather.17
  349.9 59.6 all-gather.19
  416.8 59.6 all-gather.21
  483.6 59.6 all-gather.23
  550.8 111.1 all-reduce.2
  687.8 62.4 all-gather.25
  758.5 111.1 all-reduce.4
where the time goes:
time: 888 us; the launch traced here: 880 us
  waiting for transfers between devices  767 us (86%)
  matrix products  66.2 us (7%)
  other arithmetic  23.7 us (3%)
  between operations  16.8 us (2%)
    all_gather x9, waiting for transfers between devices, apply_factor(): lax.all_gather(vectors, 'blk', axis=0, tiled=True)  544 us
    psum x1, waiting for transfers between devices, local(): lax.psum(lax.dot_general(current, current, (((0,), (0,)), ((), ())), prec...  111 us
    psum x1, waiting for transfers between devices, local(): lax.psum(lax.dot_general(basis_rows, mapped, (((0,), (0,)), ((), ())), pr...  111 us
    dot_general x10, matrix products, local_dot(): jnp.dot(left_side, right_side, precision=lax.Precision.HIGHEST, preferred...  63.3 us
  transfers between devices with their start and end apart: 11, of which 11 were waited for; matrix products, arithmetic and copies ran while one was open for 0% of the time, Pallas kernels for 0%

commit v1 on v0

--- a/solution.py
+++ b/solution.py
@@ -43,15 +43,18 @@
     cholesky_low = jnp.linalg.cholesky(gram_matrix)
     basis_rows = lower_solve(cholesky_low, current.T).T
     mapped = apply_factor(factor, basis_rows)
-    projected = lax.psum(
-        lax.dot_general(
-            basis_rows,
-            mapped,
-            (((0,), (0,)), ((), ())),
-            precision=lax.Precision.HIGHEST,
-            preferred_element_type=jnp.float32,
+    projected = jnp.sum(
+        lax.all_gather(
+            lax.dot_general(
+                basis_rows,
+                mapped,
+                (((0,), (0,)), ((), ())),
+                precision=lax.Precision.HIGHEST,
+                preferred_element_type=jnp.float32,
+            ),
+            "blk",
         ),
-        "blk",
+        axis=0,
     )
     residual = mapped - local_dot(basis_rows, projected)
     return (basis_rows, projected, residual)

time: 888 us -> 833 us (0.938)
  the two profiles are of different devices: /device:TPU:2 before, /device:TPU:32 now
where the time goes in v1:
time: 833 us; the launch traced here: 825 us
  waiting for transfers between devices  713 us (86%)
  matrix products  65.4 us (8%)
  other arithmetic  25 us (3%)
  between operations  16.8 us (2%)
    all_gather x9, waiting for transfers between devices, apply_factor(): lax.all_gather(vectors, 'blk', axis=0, tiled=True)  544 us
    psum x1, waiting for transfers between devices, local(): lax.psum(lax.dot_general(current, current, (((0,), (0,)), ((), ())), prec...  111 us
    dot_general x10, matrix products, local_dot(): jnp.dot(left_side, right_side, precision=lax.Precision.HIGHEST, preferred...  62.5 us
    all_gather x1, waiting for transfers between devices, local(): lax.all_gather(lax.dot_general(basis_rows, mapped, (((0,), (0,)), ((), ()...  56.9 us
  transfers between devices with their start and end apart: 11, of which 11 were waited for; matrix products, arithmetic and copies ran while one was open for 0% of the time, Pallas kernels for 0%

profile of v1, /device:TPU:32, one launch (start us, length us, event | category | flops | bytes accessed | tf_op | source)
XLA Modules:
  0.0 825.1 jit_solution(13330392497979138388)
XLA Ops:
  7.9 1.3 fusion.33
  11.9 63.5 %all-gather.12.cloned.1.call-done = f32[4096,128]{1,0:T(8,128)} async-done(((f32[256,128]{1,0:T(8,128)}), f32[4096,128]{1,0:T(8,128)}) %all-gather.12.cloned.1.call-update) | async-done | bytes 2097168 | tf_op jit(solution)/shard_map/all_gather | solution.py:20
  75.4 7.0 fusion.28
  82.4 59.8 %all-gather.14.cloned.1.call-done = f32[4096,128]{1,0:T(8,128)} async-done(((f32[256,128]{1,0:T(8,128)}), f32[4096,128]{1,0:T(8,128)}) %all-gather.14.cloned.1.call-update) | async-done | bytes 2097168 | tf_op jit(solution)/shard_map/all_gather | solution.py:20
  142.2 7.0 fusion.27
  149.3 59.8 %all-gather.16.cloned.1.call-done = f32[4096,128]{1,0:T(8,128)} async-done(((f32[256,128]{1,0:T(8,128)}), f32[4096,128]{1,0:T(8,128)}) %all-gather.16.cloned.1.call-update) | async-done | bytes 2097168 | tf_op jit(solution)/shard_map/all_gather | solution.py:20
  209.1 7.0 fusion.23
  216.6 59.3 %all-gather.18.cloned.1.call-done = f32[4096,128]{1,0:T(8,128)} async-done(((f32[256,128]{1,0:T(8,128)}), f32[4096,128]{1,0:T(8,128)}) %all-gather.18.cloned.1.call-update) | async-done | bytes 2097168 | tf_op jit(solution)/shard_map/all_gather | solution.py:20
  275.9 7.0 fusion.19
  283.0 59.8 %all-gather.20.cloned.1.call-done = f32[4096,128]{1,0:T(8,128)} async-done(((f32[256,128]{1,0:T(8,128)}), f32[4096,128]{1,0:T(8,128)}) %all-gather.20.cloned.1.call-update) | async-done | bytes 2097168 | tf_op jit(solution)/shard_map/all_gather | solution.py:20
  342.8 7.0 fusion.15
  349.8 59.8 %all-gather.22.cloned.1.call-done = f32[4096,128]{1,0:T(8,128)} async-done(((f32[256,128]{1,0:T(8,128)}), f32[4096,128]{1,0:T(8,128)}) %all-gather.22.cloned.1.call-update) | async-done | bytes 2097168 | tf_op jit(solution)/shard_map/all_gather | solution.py:20
  409.6 7.0 fusion.11
  416.9 59.6 %all-gather.24.cloned.1.call-done = f32[4096,128]{1,0:T(8,128)} async-done(((f32[256,128]{1,0:T(8,128)}), f32[4096,128]{1,0:T(8,128)}) %all-gather.24.cloned.1.call-update) | async-done | bytes 2097168 | tf_op jit(solution)/shard_map/all_gather | solution.py:20
  476.5 7.0 fusion.7
  483.5 59.8 %all-gather.26.cloned.1.call-done = f32[4096,128]{1,0:T(8,128)} async-done(((f32[256,128]{1,0:T(8,128)}), f32[4096,128]{1,0:T(8,128)}) %all-gather.26.cloned.1.call-update) | async-done | bytes 2097168 | tf_op jit(solution)/shard_map/all_gather | solution.py:20
  543.3 6.3 fusion.3
  551.0 111.0 %all-reduce.2.cloned.1.call-done = f32[128,128]{0,1:T(8,128)} async-done(((f32[128,128]{0,1:T(8,128)}), f32[128,128]{0,1:T(8,128)}) %all-reduce.2.cloned.1.call-update) | async-done | bytes 65552 | tf_op jit(solution)/shard_map/psum | solution.py:33
  663.8 11.7 %cholesky.16 = f32[128,128]{1,0:T(8,128)S(1)} custom-call(f32[128,128]{1,0:T(8,128)S(1)} %fusion.32), custom_call_target="Cholesky" | custom-call | tf_op jit(solution)/shard_map/jit(cholesky)/cholesky | solution.py:43
  676.8 9.8 %custom-call.6 = f32[1,128,128]{1,2,0:T(8,128)S(1)} custom-call(f32[1,128,128]{2,1,0:T(8,128)S(1)} %fusion.29), custom_call_target="InvertDiagBlocksLowerTriangular" | custom-call | tf_op jit(solution)/shard_map/triangular_solve | solution.py:16
  687.7 62.5 %all-gather.28.cloned.1.call-done = f32[4096,128]{0,1:T(8,128)} async-done(((f32[256,128]{0,1:T(8,128)}), f32[4096,128]{0,1:T(8,128)}) %all-gather.28.cloned.1.call-update) | async-done | bytes 2097168 | tf_op jit(solution)/shard_map/all_gather | solution.py:20
  750.2 7.1 fusion.35
  759.0 56.9 %all-gather.30.cloned.1.call-done = f32[2048,128]{1,0:T(8,128)} async-done(((f32[128,128]{1,0:T(8,128)}), f32[2048,128]{1,0:T(8,128)}) %all-gather.30.cloned.1.call-update) | async-done | bytes 1048592 | tf_op jit(solution)/shard_map/all_gather | solution.py:47
  816.0 1.3 reduce_sum.9
  (51 shorter events, 10.0 us)
Async XLA Ops:
  7.2 68.2 %all-gather.12.cloned.1.call-start = ((), (), s32[]{:S(2)}) async-start(), calls=%async_computation | async-start | bytes 2228224 | tf_op jit(solution)/shard_map/all_gather | solution.py:20
  7.9 134.3 %all-gather.14.cloned.1.call-start = ((), (), s32[]{:S(2)}) async-start(), calls=%async_computation.1 | async-start | bytes 2228224 | tf_op jit(solution)/shard_map/all_gather | solution.py:20
  75.4 66.9 %copy-start.7 = (f32[256,128]{1,0:T(8,128)S(1)}, f32[256,128]{1,0:T(8,128)}, u32[]{:S(2)}) copy-start(f32[256,128]{1,0:T(8,128)} %param.4) | copy-start | bytes 393220
  82.4 126.7 %copy-start.6 = (f32[256,128]{1,0:T(8,128)S(1)}, f32[256,128]{1,0:T(8,128)}, u32[]{:S(2)}) copy-start(f32[256,128]{1,0:T(8,128)} %fusion.28) | copy-start | bytes 393220
  82.4 126.7 %all-gather.16.cloned.1.call-start = ((), (), s32[]{:S(2)}) async-start(), calls=%async_computation.2 | async-start | bytes 2228224 | tf_op jit(solution)/shard_map/all_gather | solution.py:20
  149.2 126.7 %copy-start.5 = (f32[256,128]{1,0:T(8,128)S(1)}, f32[256,128]{1,0:T(8,128)}, u32[]{:S(2)}) copy-start(f32[256,128]{1,0:T(8,128)} %fusion.27) | copy-start | bytes 393220
  149.2 126.7 %all-gather.18.cloned.1.call-start = ((), (), s32[]{:S(2)}) async-start(), calls=%async_computation.3 | async-start | bytes 2228224 | tf_op jit(solution)/shard_map/all_gather | solution.py:20
  216.1 126.7 %copy-start.2 = (f32[256,128]{1,0:T(8,128)S(1)}, f32[256,128]{1,0:T(8,128)}, u32[]{:S(2)}) copy-start(f32[256,128]{1,0:T(8,128)} %fusion.23) | copy-start | bytes 393220
  216.1 126.7 %all-gather.20.cloned.1.call-start = ((), (), s32[]{:S(2)}) async-start(), calls=%async_computation.4 | async-start | bytes 2228224 | tf_op jit(solution)/shard_map/all_gather | solution.py:20
  282.9 126.7 %copy-start.3 = (f32[256,128]{1,0:T(8,128)S(1)}, f32[256,128]{1,0:T(8,128)}, u32[]{:S(2)}) copy-start(f32[256,128]{1,0:T(8,128)} %fusion.19) | copy-start | bytes 393220
  282.9 126.7 %all-gather.22.cloned.1.call-start = ((), (), s32[]{:S(2)}) async-start(), calls=%async_computation.5 | async-start | bytes 2228224 | tf_op jit(solution)/shard_map/all_gather | solution.py:20
  349.8 126.7 %copy-start.4 = (f32[256,128]{1,0:T(8,128)S(1)}, f32[256,128]{1,0:T(8,128)}, u32[]{:S(2)}) copy-start(f32[256,128]{1,0:T(8,128)} %fusion.15) | copy-start | bytes 393220
  349.8 126.7 %all-gather.24.cloned.1.call-start = ((), (), s32[]{:S(2)}) async-start(), calls=%async_computation.6 | async-start | bytes 2228224 | tf_op jit(solution)/shard_map/all_gather | solution.py:20
  416.6 126.7 %copy-start.1 = (f32[256,128]{1,0:T(8,128)S(1)}, f32[256,128]{1,0:T(8,128)}, u32[]{:S(2)}) copy-start(f32[256,128]{1,0:T(8,128)} %fusion.11) | copy-start | bytes 393220
  416.6 126.7 %all-gather.26.cloned.1.call-start = ((), (), s32[]{:S(2)}) async-start(), calls=%async_computation.7 | async-start | bytes 2228224 | tf_op jit(solution)/shard_map/all_gather | solution.py:20
  483.5 178.5 %all-reduce.2.cloned.1.call-start = ((), (), s32[]{:S(2)}) async-start(), calls=%async_computation.8 | async-start | bytes 131072 | tf_op jit(solution)/shard_map/psum | solution.py:33
  550.7 199.5 %all-gather.28.cloned.1.call-start = ((), (), s32[]{:S(2)}) async-start(), calls=%async_computation.9 | async-start | bytes 2228224 | tf_op jit(solution)/shard_map/all_gather | solution.py:20
  687.6 69.7 %copy-start = (f32[128,256]{1,0:T(8,128)S(1)}, f32[128,256]{1,0:T(8,128)}, u32[]{:S(2)}) copy-start(f32[128,256]{1,0:T(8,128)} %fusion.30) | copy-start | bytes 393220
  687.6 128.3 %all-gather.30.cloned.1.call-start = ((), (), s32[]{:S(2)}) async-start(), calls=%async_computation.10 | async-start | bytes 1114112 | tf_op jit(solution)/shard_map/all_gather | solution.py:47
  817.2 1.1 copy-start.8
Sparse Core Ops, SparseCore 0:
  11.0 64.3 all-gather.11
  82.5 59.6 all-gather.13
  149.3 59.6 all-gather.15
  216.2 59.6 all-gather.17
  283.1 59.6 all-gather.19
  349.9 59.6 all-gather.21
  416.8 59.6 all-gather.23
  483.6 59.6 all-gather.25
  550.8 111.0 all-reduce.1
  687.7 62.4 all-gather.27
  758.4 57.5 all-gather.29
